TPU v7x, 32 devices: a whole 2x2x4 slice. The times are simulated.
32 devices in a mesh: dp: 16 (over z, y, core), mp: 2 (over x).
Axes of the slice: x: 2, y: 2, z: 4, core: 2. Of those that a mesh axis runs over, the one named last changes fastest.
Arguments:
- hidden_in: bfloat16 [8192, 4096], P('dp'), may hold values from -1.5 to 1.5
- w_query: bfloat16 [4096, 4096], P('dp', 'mp'), may hold values from -1 to 1
- w_key: bfloat16 [4096, 1024], P('dp', 'mp'), may hold values from -24 to 24
- w_value: bfloat16 [4096, 1024], P('dp', 'mp'), may hold values from -1 to 1
- w_out: bfloat16 [4096, 4096], P('dp', 'mp'), may hold values from -1 to 1
- value_weight: float32 [4096], P('mp'), may hold values from -0.09375 to 0.09375
- rewards: float32 [8192], P('dp'), may hold values from -0.6 to 0.6
- old_values: float32 [8192], P('dp'), may hold values from -6 to 6
- lengths: int32 [64], replicated, may hold values from 1 to 2048, 8192 in all
- terminal: int32 [64], replicated, may hold values 0 or 1
Outputs:
- value: float32 [8192], P('dp')
- advantage: float32 [8192], P('dp')
- value_loss: float32 [], replicated
All inputs are finite; a program needn't handle non-finite values.
Results may differ from a plain program's by a relative error of at most 0.012.
The roundings to bfloat16 on the way count: a program that leaves them out, or rounds other values in their place, can miss the bound.
Values may be sent and summed in bfloat16 or wider, within the bound.
No kernel may reach another device: no remote copies, remote signals or barrier semaphores. Data moves between devices by JAX's collectives and lax.ppermute only.
A program may use at most 128 MiB of HBM per device.

v0:
```python
import jax
import jax.numpy as jnp
from jax import lax
from jax.sharding import PartitionSpec as P

HEAD = 128
discount = 0.999
trace_decay = 0.997
clip_range = 0.2
epsilon = 1e-05
rope_base = 500000.0


def from_behind(array, axis, by):
    size = lax.axis_size(axis)
    pairs = [(i, i + by) for i in range(size) if 0 <= i + by < size]
    return lax.ppermute(array, axis, pairs)


def carried_in(part, axis, combine, identity):
    count = lax.axis_size(axis)
    place = lax.axis_index(axis)
    ahead = count - 1 - place
    gathered = jax.tree.map(lambda a: lax.all_gather(a, axis), part)
    state = jax.tree.map(lambda a, e: jnp.zeros_like(a) + jnp.asarray(e, a.dtype), part, identity)

    def one(hop, state):
        source = count - 1 - hop
        return combine(
            state, jax.tree.map(lambda a: lax.dynamic_index_in_dim(a, source, 0, False), gathered)
        )

    return lax.fori_loop(0, ahead, one, state)


def rotate(states, positions):
    half = HEAD // 2
    freq = rope_base ** (-jnp.arange(half, dtype=jnp.float32) * 2.0 / HEAD)
    angles = positions[:, None] * freq[None, :]
    cosine = jnp.cos(angles)[:, None, :]
    sine = jnp.sin(angles)[:, None, :]
    first = states[..., :half]
    second = states[..., half:]
    return jnp.concatenate([first * cosine - second * sine, second * cosine + first * sine], -1)


def body(
    hidden_in, w_query, w_key, w_value, w_out, value_weight, rewards, old_values, lengths, terminal
):
    rows = hidden_in.shape[0]
    width = hidden_in.shape[1]
    states = hidden_in.astype(jnp.float32)
    normed = (states * lax.rsqrt(jnp.mean(states * states, 1, keepdims=True) + epsilon)).astype(
        jnp.bfloat16
    )
    pieces = (
        lax.all_gather(w_query, "dp", axis=0, tiled=True),
        lax.all_gather(w_key, "dp", axis=0, tiled=True),
        lax.all_gather(w_value, "dp", axis=0, tiled=True),
        lax.all_gather(w_out, "dp", axis=0, tiled=True),
    )
    add_pieces = pieces[:3]
    summed = tuple(
        (jnp.dot(normed, piece, preferred_element_type=jnp.float32) for piece in add_pieces)
    )
    stored = pieces[3]
    query_sum, key_sum, value_sum, whole_out = summed + (stored,)
    position_ids = lax.axis_index("dp") * rows + jnp.arange(rows, dtype=jnp.int32)
    positions = position_ids.astype(jnp.float32)
    local_heads = w_query.shape[1] // HEAD
    local_kv = w_key.shape[1] // HEAD
    group = local_heads // local_kv
    query = rotate(query_sum.reshape(rows, local_heads, HEAD), positions).astype(jnp.bfloat16)
    key = rotate(key_sum.reshape(rows, local_kv, HEAD), positions).astype(jnp.bfloat16)
    values_proj = value_sum.astype(jnp.bfloat16).reshape(rows, local_kv, HEAD)
    ends = jnp.cumsum(lengths)
    matches = ends[None, :] - 1 == position_ids[:, None]
    finished = jnp.any(matches, 1).astype(jnp.float32)
    stopped = jnp.sum(jnp.where(matches, terminal[None, :], 0), 1).astype(jnp.float32)
    episode = jnp.sum((ends[None, :] <= position_ids[:, None]).astype(jnp.int32), 1)
    order = jnp.arange(rows, dtype=jnp.int32)
    same_episode = episode[None, :] == episode[:, None]
    allowed = (order[None, :] <= order[:, None]) & same_episode
    scores = jnp.einsum(
        "tkgd,skd->kgts",
        query.reshape(rows, local_kv, group, HEAD),
        key,
        preferred_element_type=jnp.float32,
    ) * (1.0 / HEAD**0.5)
    masked = jnp.where(allowed[None, None], scores, -1e30)
    largest = jnp.max(masked, -1, keepdims=True)
    expon = jnp.where(allowed[None, None], jnp.exp(masked - largest), 0.0)
    probs = (expon / jnp.sum(expon, -1, keepdims=True)).astype(jnp.bfloat16)
    output = jnp.einsum("kgts,skd->tkgd", probs, values_proj, preferred_element_type=jnp.float32)
    attended = output.astype(jnp.bfloat16).reshape(rows, local_heads * HEAD)
    all_heads = lax.all_gather(attended, "mp", axis=1, tiled=True)
    projected = jnp.dot(all_heads, whole_out, preferred_element_type=jnp.float32)
    feature_count = w_out.shape[1]
    own_states = lax.dynamic_slice_in_dim(
        states, lax.axis_index("mp") * feature_count, feature_count, 1
    )
    residual = own_states + projected
    square_sum, head_sum = lax.psum(
        (jnp.sum(residual * residual, 1), jnp.sum(residual * value_weight[None, :], 1)), "mp"
    )
    value = head_sum * lax.rsqrt(square_sum / width + epsilon)
    following = from_behind(old_values[:1], "dp", -1)
    next_old = jnp.concatenate([old_values[1:], following])
    booted = jnp.where(finished > 0, (1.0 - stopped) * old_values, next_old)
    delta = rewards + discount * booted - old_values
    keep_rate = discount * trace_decay
    spacing = (order[None, :] - order[:, None]).astype(jnp.float32)
    forward_mask = (spacing >= 0.0) & same_episode
    decay_matrix = jnp.where(
        forward_mask, jnp.power(jnp.float32(keep_rate), jnp.maximum(spacing, 0.0)), 0.0
    )
    local_part = jnp.dot(decay_matrix, delta, precision=lax.Precision.HIGHEST)
    remaining = (rows - order).astype(jnp.float32)
    reach = jnp.where(episode == episode[-1], jnp.power(jnp.float32(keep_rate), remaining), 0.0) * (
        1.0 - finished[-1]
    )

    def compose(earlier, later_map):
        return (later_map[0] + later_map[1] * earlier[0], later_map[1] * earlier[1])

    prefix = carried_in(
        (local_part[:1], reach[:1]),
        "dp",
        compose,
        (jnp.zeros((1,), jnp.float32), jnp.ones((1,), jnp.float32)),
    )
    incoming = prefix[0][0]
    advantage = local_part + reach * incoming
    returns = advantage + old_values
    clipped = old_values + jnp.clip(value - old_values, -clip_range, clip_range)
    terms = jnp.maximum((value - returns) ** 2, (clipped - returns) ** 2)
    total_loss = lax.psum(jnp.sum(terms), "dp")
    value_loss = 0.5 * total_loss / (rows * lax.axis_size("dp"))
    return (value, advantage, value_loss)


def solution(mesh):
    return jax.shard_map(
        body,
        mesh=mesh,
        in_specs=(
            P("dp", None),
            P("dp", "mp"),
            P("dp", "mp"),
            P("dp", "mp"),
            P("dp", "mp"),
            P("mp"),
            P("dp"),
            P("dp"),
            P(),
            P(),
        ),
        out_specs=(P("dp"), P("dp"), P()),
        check_vma=False,
    )
```

profile of v0, /device:TPU:0, one launch (start us, length us, event | category | flops | bytes accessed | tf_op | source)
XLA Modules:
  0.0 487.3 jit_solution(12846572343256018310)
XLA Ops:
  7.2 0.7 all-gather.10.cloned.1.call-update
  7.9 0.7 all-gather.8.cloned.1.call-update
  8.7 0.7 all-gather.12.cloned.1.call-update
  10.0 0.7 copy.25
  11.0 0.8 fusion.22
  11.8 3.1 multiply_reduce_fusion
  15.1 1.0 multiply_cosine_fusion
  16.1 47.2 %all-gather.10.cloned.1.call-done = bf16[4096,512]{1,0:T(8,128)(2,1)} async-done(((bf16[256,512]{1,0:T(8,128)(2,1)}), bf16[4096,512]{1,0:T(8,128)(2,1)}) %all-gather.10.cloned.1.call-update) | async-done | bytes 4194320 | tf_op jit(solution)/shard_map/all_gather | solution.py:58
  63.3 5.9 %fusion.32 = f32[512,512]{0,1:T(8,128)S(1)} fusion(bf16[4096,512]{1,0:T(8,128)(2,1)} %all-gather.10.cloned.1.call-done, f32[512]{0:T(512)S(1)} %add_rsqrt_fusion, bf16[512,4096]{1,0:T(8,128)(2,1)} %param.12), kind=kOutput, calls=%fused_computation.70 | convolution fusion | flops 2153775104 | bytes 9439232 | tf_op jit(solution)/shard_map/dot_general | solution.py:64
  69.9 1.1 subtract_convert_fusion.1
  71.0 43.3 %all-gather.8.cloned.1.call-done = bf16[4096,512]{1,0:T(8,128)(2,1)} async-done(((bf16[256,512]{1,0:T(8,128)(2,1)}), bf16[4096,512]{1,0:T(8,128)(2,1)}) %all-gather.8.cloned.1.call-update) | async-done | bytes 4194320 | tf_op jit(solution)/shard_map/all_gather | solution.py:59
  114.4 5.9 %convolution_convert_fusion = bf16[512,512]{0,1:T(8,128)(2,1)S(1)} fusion(bf16[4096,512]{1,0:T(8,128)(2,1)} %all-gather.8.cloned.1.call-done, f32[512]{0:T(512)S(1)} %add_rsqrt_fusion, bf16[512,4096]{1,0:T(8,128)(2,1)} %param.12), kind=kOutput, calls=%fused_computation.26 | convolution fusion | flops 2154037248 | bytes 8914944 | tf_op jit(solution)/shard_map/dot_general | solution.py:64
  120.3 121.2 %all-gather.12.cloned.1.call-done = bf16[4096,2048]{1,0:T(8,128)(2,1)} async-done(((bf16[256,2048]{1,0:T(8,128)(2,1)}), bf16[4096,2048]{1,0:T(8,128)(2,1)}) %all-gather.12.cloned.1.call-update) | async-done | bytes 16777232 | tf_op jit(solution)/shard_map/all_gather | solution.py:57
  241.5 13.2 %convolution_bitcast_fusion = f32[64,8,16,128]{3,1,2,0:T(8,128)S(1)} fusion(bf16[4096,2048]{1,0:T(8,128)(2,1)} %all-gather.12.cloned.1.call-done, f32[512]{0:T(512)S(1)} %add_rsqrt_fusion, bf16[512,4096]{1,0:T(8,128)(2,1)} %param.12), kind=kOutput, calls=%fused_computation.18 | convolution fusion | flops 8596226048 | bytes 25167872 | tf_op jit(solution)/shard_map/dot_general | solution.py:64
  254.8 0.9 copy.36
  255.7 1.8 subtract_convert_fusion
  258.6 8.1 %fusion.6 = f32[4,512,512,4]{2,1,3,0:T(8,128)} fusion(bf16[512,4,4,64]{3,0,2,1:T(8,128)(2,1)S(1)} %bitcast.53, bf16[512,4,4,64]{3,0,2,1:T(8,128)(2,1)S(1)} %bitcast.54, bf16[512,4,64]{2,0,1:T(8,128)(2,1)S(1)} %copy-done, bf16[512,4,64]{2,0,1:T(8,128)(2,1)S(1)} %get-tuple-element.113), kind=kOutput, calls=%fused_computation.19 | convolution fusion | flops 1078984704 | bytes 19398656 | tf_op jit(solution)/shard_map/tkgd,skd->kgts/dot_general | solution.py:84
  266.8 17.9 %fusion.34 = (f32[4,4,512]{2,1,0:T(4,128)S(1)}, f32[4,4,512,512]{2,3,1,0:T(8,128)}) fusion(f32[4,512,512,4]{2,1,3,0:T(8,128)} %fusion.6, pred[512,512]{0,1:T(8,128)(4,1)S(1)} %compare_and_fusion.1), kind=kOutput, calls=%fused_computation.72 | output fusion | flops 29360640 | bytes 33849344 | tf_op jit(solution)/shard_map/sub | solution.py:92
  284.7 8.6 %fusion.10 = bf16[4,128,4,512]{3,1,2,0:T(8,128)(2,1)} fusion(bf16[512,4,128,1]{0,2,3,1:T(8,128)(2,1)S(1)} %bitcast.63, f32[4,4,512,512]{2,3,1,0:T(8,128)} %get-tuple-element.120, f32[4,4,512]{2,1,0:T(4,128)S(1)} %get-tuple-element.119), kind=kOutput, calls=%fused_computation.23 | convolution fusion | flops 1083179008 | bytes 19431424 | tf_op jit(solution)/shard_map/kgts,skd->tkgd/dot_general | solution.py:94
  293.9 1.3 collective-permute-start
  295.2 6.5 %convert_element_type.45 = f32[512,4096]{1,0:T(8,128)} convert(bf16[512,4096]{1,0:T(8,128)(2,1)} %param.12) | non-fusion elementwise | flops 2097152 | bytes 12582912 | tf_op jit(solution)/shard_map/convert_element_type | solution.py:52
  305.1 0.7 slice_dynamic-update-slice_fusion
  305.8 0.7 fusion.25
  306.5 1.1 fusion.11
  307.6 0.7 slice_dynamic-update-slice_fusion.1
  308.3 34.8 %all-reduce.2 = (f32[16]{0:T(128)S(1)}, f32[16]{0:T(128)S(1)}) all-reduce(f32[16]{0:T(128)S(1)} %slice_dynamic-update-slice_fusion.1, f32[16]{0:T(128)S(1)} %slice_dynamic-update-slice_fusion), channel_id=2, replica_groups=mesh['dp'=16,'mp'=2] {'dp'}, use_global_device_ids=true, to_apply=%add | all-reduce | flops 32 | bytes 256
  343.1 28.6 %while.14 = (s32[]{:T(128)}, f32[1]{0:T(128)}, s32[]{:T(128)}, f32[16,1]{0,1:T(1,128)S(1)}, f32[16,1]{0,1:T(1,128)S(1)}, /*index=5*/s32[]{:T(128)}, s32[]{:T(128)}, s32[]{:T(128)}, s32[]{:T(128)}) while((s32[]{:T(128)}, f32[1]{0:T(128)}, s32[]{:T(128)}, f32[16,1]{0,1:T(1,128)S(1)}, f32[16,1]{0,1:T(1,128)S(1)}, /*index=5*/s32[]{:T(128)}, ...), condition=%wide.region_12.13_spmd, body=%wide.region_11.12_spmd.sunk | while | flops 8 | bytes 183 | solution.py:33
  371.7 53.4 %all-gather.14.cloned.1.call-done = bf16[512,4096]{0,1:T(8,128)(2,1)} async-done(((bf16[512,2048]{0,1:T(8,128)(2,1)}), bf16[512,4096]{0,1:T(8,128)(2,1)}) %all-gather.14.cloned.1.call-update) | async-done | bytes 4194320 | tf_op jit(solution)/shard_map/all_gather | solution.py:96
  425.1 14.6 %multiply_reduce_fusion.1 = (f32[512]{0:T(512)S(1)}, f32[512]{0:T(512)S(1)}) fusion(f32[2048]{0:T(1024)S(1)} %copy-done.3, bf16[512,4096]{0,1:T(8,128)(2,1)} %all-gather.14.cloned.1.call-done, bf16[4096,2048]{1,0:T(8,128)(2,1)} %all-gather.16.cloned.1.call-done, f32[512,4096]{1,0:T(8,128)} %convert_element_type.45, s32[]{:T(128)S(6)} %select_n.35), kind=kOutput, calls=%fused_computation.13 | convolution fusion | flops 8595177472 | bytes 25178116 | tf_op jit(solution)/shard_map/dot_general | solution.py:97
  439.7 4.9 %all-reduce.3 = (f32[512]{0:T(512)S(1)}, f32[512]{0:T(512)S(1)}) all-reduce(f32[512]{0:T(512)S(1)} %get-tuple-element.89, f32[512]{0:T(512)S(1)} %get-tuple-element.88), channel_id=1, replica_groups=mesh['dp'=16,'mp'=2] {'mp'}, use_global_device_ids=true, to_apply=%region_6.7 | all-reduce | flops 1024 | bytes 8192 | tf_op jit(solution)/shard_map/psum | solution.py:103
  444.7 1.9 maximum_reduce_fusion
  446.5 32.5 %psum.23 = f32[]{:T(128)} all-reduce(f32[]{:T(128)} %get-tuple-element.106), channel_id=1, replica_groups=mesh['dp'=16,'mp'=2] {'dp'}, use_global_device_ids=true, to_apply=%region_14.15 | all-reduce | flops 1 | bytes 8 | tf_op jit(solution)/shard_map/psum | solution.py:137
  (57 shorter events, 15.6 us)
Async XLA Ops:
  7.2 56.1 %all-gather.10.cloned.1.call-start = ((), (), s32[]{:S(2)}) async-start(), calls=%async_computation.1 | async-start | bytes 4456448 | tf_op jit(solution)/shard_map/all_gather | solution.py:58
  7.9 106.5 %all-gather.8.cloned.1.call-start = ((), (), s32[]{:S(2)}) async-start(), calls=%async_computation | async-start | bytes 4456448 | tf_op jit(solution)/shard_map/all_gather | solution.py:59
  8.7 232.9 %all-gather.12.cloned.1.call-start = ((), (), s32[]{:S(2)}) async-start(), calls=%async_computation.2 | async-start | bytes 17825792 | tf_op jit(solution)/shard_map/all_gather | solution.py:57
  9.4 362.3 %all-gather.16.cloned.1.call-start = ((), (), s32[]{:S(2)}) async-start(), calls=%async_computation.4 | async-start | bytes 17825792 | tf_op jit(solution)/shard_map/all_gather | solution.py:60
  10.0 415.2 %all-gather.14.cloned.1.call-start = ((), (), s32[]{:S(2)}) async-start(), calls=%async_computation.3 | async-start | bytes 6291456 | tf_op jit(solution)/shard_map/all_gather | solution.py:96
  257.5 1.1 copy-start
  284.7 8.6 %copy-start.1 = (f32[512]{0:T(512)S(1)}, f32[512]{0:T(512)}, u32[]{:S(2)}) copy-start(f32[512]{0:T(512)} %param.19) | copy-start | bytes 6148
  293.9 12.0 %collective-permute-start = (f32[1]{0:T(128)}, f32[1]{0:T(128)}, u32[]{:S(2)}, u32[]{:S(2)}) collective-permute-start(f32[1]{0:T(128)} %slice.35), channel_id=1, source_target_pairs={{2,0},{4,2},{6,4},{8,6},{10,8},{12,10},{14,12},{16,14},{18,16},{20... | collective-permute-start | bytes 20 | tf_op jit(solution)/shard_map/ppermute | solution.py:17
  295.2 8.6 %copy-start.4 = (u32[32]{0:T(128)S(1)}, u32[32]{0:T(128)}, u32[]{:S(2)}) copy-start(u32[32]{0:T(128)} %constant.106) | copy-start | bytes 388
  295.2 10.7 %copy-start.2 = (f32[512]{0:T(512)S(1)}, f32[512]{0:T(512)}, u32[]{:S(2)}) copy-start(f32[512]{0:T(512)} %param.18) | copy-start | bytes 6148
  295.2 130.0 %copy-start.3 = (f32[2048]{0:T(1024)S(1)}, f32[2048]{0:T(1024)}, u32[]{:S(2)}) copy-start(f32[2048]{0:T(1024)} %param.17) | copy-start | bytes 24580
Sparse Core Ops, SparseCore 0:
  10.1 53.0 all-gather.9
  65.4 48.8 all-gather.7
  116.5 124.9 all-gather.11
  243.6 125.2 all-gather.15
  370.2 54.8 all-gather.13
where the time goes:
time: 488 us; the launch traced here: 487 us
  waiting for transfers between devices  268 us (55%)
  blocking collectives  72.2 us (15%)
  matrix products  57.5 us (12%)
  other arithmetic  36 us (7%)
  loops' own time  19.3 us (4%)
  local copies, waits for them, and re-layouts  16.7 us (3%)
  between operations  16.4 us (3%)
    all_gather x1, waiting for transfers between devices, body(): lax.all_gather(w_query, 'dp', axis=0, tiled=True)  121 us
    all_gather x1, waiting for transfers between devices, body(): all_heads = lax.all_gather(attended, 'mp', axis=1, tiled=True)  53.4 us
    all_gather x1, waiting for transfers between devices, body(): lax.all_gather(w_key, 'dp', axis=0, tiled=True)  47.2 us
    all_gather x1, waiting for transfers between devices, body(): lax.all_gather(w_value, 'dp', axis=0, tiled=True)  43.3 us
    unnamed x1, blocking collectives  34.8 us
    psum x1, blocking collectives, body(): total_loss = lax.psum(jnp.sum(terms), 'dp')  32.5 us
    dot_general x3, matrix products, body(): jnp.dot(normed, piece, preferred_element_type=jnp.float32)  25 us
    another operation x1, loops' own time, carried_in(): return lax.fori_loop(0, ahead, one, state)  19.3 us
  transfers between devices with their start and end apart: 6, of which 4 were waited for; matrix products, arithmetic and copies ran while one was open for 19% of the time, Pallas kernels for 0%

commit v1 on v0

--- a/solution.py
+++ b/solution.py
@@ -9,6 +9,21 @@
 clip_range = 0.2
 epsilon = 1e-05
 rope_base = 500000.0
+
+
+def _list_layers_all(in_dim, local_array):
+    net_axis = "mp"
+    field_out, newest = (lax.axis_size(net_axis), lax.axis_index(net_axis))
+    all_values, r1 = (local_array, 1)
+    while r1 < field_out:
+        last = lax.ppermute(
+            all_values, axis_name=net_axis, perm=[(s, s ^ r1) for s in range(field_out)]
+        )
+        spare = jnp.concatenate([all_values, last], axis=in_dim)
+        local_now = jnp.concatenate([last, all_values], in_dim)
+        all_values = jnp.where(newest & r1 == 0, spare, local_now)
+        r1 = 2 * r1
+    return all_values
 
 
 def from_behind(array, axis, by):
@@ -93,7 +108,7 @@
     probs = (expon / jnp.sum(expon, -1, keepdims=True)).astype(jnp.bfloat16)
     output = jnp.einsum("kgts,skd->tkgd", probs, values_proj, preferred_element_type=jnp.float32)
     attended = output.astype(jnp.bfloat16).reshape(rows, local_heads * HEAD)
-    all_heads = lax.all_gather(attended, "mp", axis=1, tiled=True)
+    all_heads = _list_layers_all(1, attended)
     projected = jnp.dot(all_heads, whole_out, preferred_element_type=jnp.float32)
     feature_count = w_out.shape[1]
     own_states = lax.dynamic_slice_in_dim(

time: 488 us -> 437 us (0.90)
  waiting for transfers between devices: 268 us -> 214 us
    all_gather x1 -> x0, waiting for transfers between devices: 53.4 us -> none  [body(): all_heads = lax.all_gather(attended, 'mp', axis=1, tiled=True)]
  transfers between devices with their start and end apart: 6 -> 6, of which waited for: 4 -> 3; matrix products, arithmetic and copies ran while one was open for 19% -> 21% of each run, Pallas kernels for 0% -> 0%
where the time goes in v1:
time: 437 us; the launch traced here: 436 us
  waiting for transfers between devices  214 us (49%)
  blocking collectives  70.1 us (16%)
  matrix products  59 us (14%)
  other arithmetic  35.6 us (8%)
  loops' own time  20.2 us (5%)
  local copies, waits for them, and re-layouts  17.2 us (4%)
  between operations  16.4 us (4%)
    all_gather x1, waiting for transfers between devices, body(): lax.all_gather(w_query, 'dp', axis=0, tiled=True)  121 us
    all_gather x1, waiting for transfers between devices, body(): lax.all_gather(w_key, 'dp', axis=0, tiled=True)  47.2 us
    all_gather x1, waiting for transfers between devices, body(): lax.all_gather(w_value, 'dp', axis=0, tiled=True)  43.3 us
    unnamed x1, blocking collectives  35.1 us
    psum x1, blocking collectives, body(): total_loss = lax.psum(jnp.sum(terms), 'dp')  30.1 us
    dot_general x3, matrix products, body(): jnp.dot(normed, piece, preferred_element_type=jnp.float32)  25 us
    another operation x1, loops' own time, carried_in(): return lax.fori_loop(0, ahead, one, state)  20.2 us
    sub x1, other arithmetic, body(): expon = jnp.where(allowed[None, None], jnp.exp(masked - largest), 0.0)  17.9 us
  transfers between devices with their start and end apart: 6, of which 3 were waited for; matrix products, arithmetic and copies ran while one was open for 21% of the time, Pallas kernels for 0%

profile of v1, /device:TPU:0, one launch (start us, length us, event | category | flops | bytes accessed | tf_op | source)
XLA Modules:
  0.0 435.9 jit_solution(8704063032176392789)
XLA Ops:
  7.2 0.7 all-gather.9.cloned.1.call-update
  7.9 0.7 all-gather.7.cloned.1.call-update
  8.7 0.7 all-gather.11.cloned.1.call-update
  10.0 0.7 copy.25
  11.0 0.8 fusion.29
  11.7 3.1 multiply_reduce_fusion
  15.1 1.0 multiply_cosine_fusion
  16.0 47.2 %all-gather.9.cloned.1.call-done = bf16[4096,512]{1,0:T(8,128)(2,1)} async-done(((bf16[256,512]{1,0:T(8,128)(2,1)}), bf16[4096,512]{1,0:T(8,128)(2,1)}) %all-gather.9.cloned.1.call-update) | async-done | bytes 4194320 | tf_op jit(solution)/shard_map/all_gather | solution.py:73
  63.3 5.9 %fusion.40 = f32[512,512]{0,1:T(8,128)S(1)} fusion(bf16[4096,512]{1,0:T(8,128)(2,1)} %all-gather.9.cloned.1.call-done, f32[512]{0:T(512)S(1)} %add_rsqrt_fusion, bf16[512,4096]{1,0:T(8,128)(2,1)} %param.12), kind=kOutput, calls=%fused_computation.79 | convolution fusion | flops 2153775104 | bytes 9439232 | tf_op jit(solution)/shard_map/dot_general | solution.py:79
  70.0 1.1 subtract_convert_fusion.1
  71.0 43.3 %all-gather.7.cloned.1.call-done = bf16[4096,512]{1,0:T(8,128)(2,1)} async-done(((bf16[256,512]{1,0:T(8,128)(2,1)}), bf16[4096,512]{1,0:T(8,128)(2,1)}) %all-gather.7.cloned.1.call-update) | async-done | bytes 4194320 | tf_op jit(solution)/shard_map/all_gather | solution.py:74
  114.4 5.9 %convolution_convert_fusion = bf16[512,512]{0,1:T(8,128)(2,1)S(1)} fusion(bf16[4096,512]{1,0:T(8,128)(2,1)} %all-gather.7.cloned.1.call-done, f32[512]{0:T(512)S(1)} %add_rsqrt_fusion, bf16[512,4096]{1,0:T(8,128)(2,1)} %param.12), kind=kOutput, calls=%fused_computation.34 | convolution fusion | flops 2154037248 | bytes 8914944 | tf_op jit(solution)/shard_map/dot_general | solution.py:79
  120.3 121.2 %all-gather.11.cloned.1.call-done = bf16[4096,2048]{1,0:T(8,128)(2,1)} async-done(((bf16[256,2048]{1,0:T(8,128)(2,1)}), bf16[4096,2048]{1,0:T(8,128)(2,1)}) %all-gather.11.cloned.1.call-update) | async-done | bytes 16777232 | tf_op jit(solution)/shard_map/all_gather | solution.py:72
  241.5 13.2 %convolution_bitcast_fusion = f32[64,8,16,128]{3,1,2,0:T(8,128)S(1)} fusion(bf16[4096,2048]{1,0:T(8,128)(2,1)} %all-gather.11.cloned.1.call-done, f32[512]{0:T(512)S(1)} %add_rsqrt_fusion, bf16[512,4096]{1,0:T(8,128)(2,1)} %param.12), kind=kOutput, calls=%fused_computation.26 | convolution fusion | flops 8596226048 | bytes 25167872 | tf_op jit(solution)/shard_map/dot_general | solution.py:79
  254.7 0.9 copy.36
  255.7 1.7 subtract_convert_fusion
  258.5 8.1 %fusion.13 = f32[4,512,512,4]{2,1,3,0:T(8,128)} fusion(bf16[512,4,4,64]{3,0,2,1:T(8,128)(2,1)S(1)} %bitcast.52, bf16[512,4,4,64]{3,0,2,1:T(8,128)(2,1)S(1)} %bitcast.53, bf16[512,4,64]{2,0,1:T(8,128)(2,1)S(1)} %copy-done, bf16[512,4,64]{2,0,1:T(8,128)(2,1)S(1)} %get-tuple-element.113), kind=kOutput, calls=%fused_computation.27 | convolution fusion | flops 1078984704 | bytes 19398656 | tf_op jit(solution)/shard_map/tkgd,skd->kgts/dot_general | solution.py:99
  266.6 17.9 %fusion.42 = (f32[4,4,512]{2,1,0:T(4,128)S(1)}, f32[4,4,512,512]{2,3,1,0:T(8,128)}) fusion(f32[4,512,512,4]{2,1,3,0:T(8,128)} %fusion.13, pred[512,512]{0,1:T(8,128)(4,1)S(1)} %compare_and_fusion.1), kind=kOutput, calls=%fused_computation.81 | output fusion | flops 29360640 | bytes 33849344 | tf_op jit(solution)/shard_map/sub | solution.py:107
  284.5 7.1 %fusion.17 = bf16[4,128,4,512]{3,1,2,0:T(8,128)(2,1)S(1)} fusion(bf16[512,4,128,1]{0,2,3,1:T(8,128)(2,1)S(1)} %bitcast.63, f32[4,4,512,512]{2,3,1,0:T(8,128)} %get-tuple-element.120, f32[4,4,512]{2,1,0:T(4,128)S(1)} %get-tuple-element.119), kind=kOutput, calls=%fused_computation.31 | convolution fusion | flops 1083179008 | bytes 19431424 | tf_op jit(solution)/shard_map/kgts,skd->tkgd/dot_general | solution.py:109
  291.6 1.5 collective-permute-start
  293.6 1.3 collective-permute-start.1
  294.9 6.5 %convert_element_type.45 = f32[512,4096]{1,0:T(8,128)} convert(bf16[512,4096]{1,0:T(8,128)(2,1)} %param.12) | non-fusion elementwise | flops 2097152 | bytes 12582912 | tf_op jit(solution)/shard_map/convert_element_type | solution.py:67
  304.5 0.8 slice_dynamic-update-slice_fusion
  305.3 0.8 fusion.32
  306.1 1.1 fusion.18
  307.2 0.8 slice_dynamic-update-slice_fusion.1
  307.9 35.1 %all-reduce.2 = (f32[16]{0:T(128)S(1)}, f32[16]{0:T(128)S(1)}) all-reduce(f32[16]{0:T(128)S(1)} %slice_dynamic-update-slice_fusion.1, f32[16]{0:T(128)S(1)} %slice_dynamic-update-slice_fusion), channel_id=2, replica_groups=mesh['dp'=16,'mp'=2] {'dp'}, use_global_device_ids=true, to_apply=%add | all-reduce | flops 32 | bytes 256
  343.0 30.0 %while.14 = (s32[]{:T(128)}, f32[1]{0:T(128)}, s32[]{:T(128)}, f32[16,1]{0,1:T(1,128)S(1)}, f32[16,1]{0,1:T(1,128)S(1)}, /*index=5*/s32[]{:T(128)}, s32[]{:T(128)}, s32[]{:T(128)}, s32[]{:T(128)}) while((s32[]{:T(128)}, f32[1]{0:T(128)}, s32[]{:T(128)}, f32[16,1]{0,1:T(1,128)S(1)}, f32[16,1]{0,1:T(1,128)S(1)}, /*index=5*/s32[]{:T(128)}, ...), condition=%wide.region_12.13_spmd, body=%wide.region_11.12_spmd.sunk | while | flops 8 | bytes 183 | solution.py:48
  373.1 17.6 %multiply_reduce_fusion.1 = (f32[512]{0:T(512)S(1)}, f32[512]{0:T(512)S(1)}) fusion(f32[2048]{0:T(1024)S(1)} %copy-done.3, bf16[4096,2048]{1,0:T(8,128)(2,1)} %all-gather.13.cloned.1.call-done, bf16[512,2048]{0,1:T(8,128)(2,1)} %collective-permute-done, bf16[512,2048]{0,1:T(8,128)(2,1)S(1)} %bitcast.62, pred[]{:T(512)S(6)} %eq.37, ...), kind=kOutput, calls=%fused_computation.20 | convolution fusion | flops 8614051840 | bytes 25178116 | tf_op jit(solution)/shard_map/dot_general | solution.py:112
  390.8 4.9 %all-reduce.3 = (f32[512]{0:T(512)S(1)}, f32[512]{0:T(512)S(1)}) all-reduce(f32[512]{0:T(512)S(1)} %get-tuple-element.89, f32[512]{0:T(512)S(1)} %get-tuple-element.88), channel_id=1, replica_groups=mesh['dp'=16,'mp'=2] {'mp'}, use_global_device_ids=true, to_apply=%region_6.7 | all-reduce | flops 1024 | bytes 8192 | tf_op jit(solution)/shard_map/psum | solution.py:118
  395.7 1.7 maximum_reduce_fusion
  397.5 30.1 %psum.23 = f32[]{:T(128)} all-reduce(f32[]{:T(128)} %get-tuple-element.106), channel_id=1, replica_groups=mesh['dp'=16,'mp'=2] {'dp'}, use_global_device_ids=true, to_apply=%region_14.15 | all-reduce | flops 1 | bytes 8 | tf_op jit(solution)/shard_map/psum | solution.py:152
  (56 shorter events, 15.8 us)
Async XLA Ops:
  7.2 56.1 %all-gather.9.cloned.1.call-start = ((), (), s32[]{:S(2)}) async-start(), calls=%async_computation.1 | async-start | bytes 4456448 | tf_op jit(solution)/shard_map/all_gather | solution.py:73
  7.9 106.5 %all-gather.7.cloned.1.call-start = ((), (), s32[]{:S(2)}) async-start(), calls=%async_computation | async-start | bytes 4456448 | tf_op jit(solution)/shard_map/all_gather | solution.py:74
  8.7 232.9 %all-gather.11.cloned.1.call-start = ((), (), s32[]{:S(2)}) async-start(), calls=%async_computation.2 | async-start | bytes 17825792 | tf_op jit(solution)/shard_map/all_gather | solution.py:72
  9.4 363.7 %all-gather.13.cloned.1.call-start = ((), (), s32[]{:S(2)}) async-start(), calls=%async_computation.3 | async-start | bytes 17825792 | tf_op jit(solution)/shard_map/all_gather | solution.py:75
  257.4 1.1 copy-start
  284.5 8.5 %copy-start.1 = (f32[512]{0:T(512)S(1)}, f32[512]{0:T(512)}, u32[]{:S(2)}) copy-start(f32[512]{0:T(512)} %param.19) | copy-start | bytes 6148
  291.6 81.5 %collective-permute-start = (bf16[512,2048]{0,1:T(8,128)(2,1)S(1)}, bf16[512,2048]{0,1:T(8,128)(2,1)}, u32[]{:S(2)}, u32[]{:S(2)}) collective-permute-start(bf16[512,2048]{0,1:T(8,128)(2,1)S(1)} %bitcast.61), channel_id=1, source_target_pairs={{0,1},{1,0},{2,3},{3,2},{4,5},{5,4},{6,7},{7,6},{8,9},{9,8},{10,11... | collective-permute-start | bytes 6291464 | tf_op jit(solution)/shard_map/ppermute | solution.py:19
  293.6 11.7 %collective-permute-start.1 = (f32[1]{0:T(128)}, f32[1]{0:T(128)}, u32[]{:S(2)}, u32[]{:S(2)}) collective-permute-start(f32[1]{0:T(128)} %slice.35), channel_id=1, source_target_pairs={{2,0},{4,2},{6,4},{8,6},{10,8},{12,10},{14,12},{16,14},{18,16},{20... | collective-permute-start | bytes 20 | tf_op jit(solution)/shard_map/ppermute | solution.py:32
  294.9 8.4 %copy-start.4 = (u32[32]{0:T(128)S(1)}, u32[32]{0:T(128)}, u32[]{:S(2)}) copy-start(u32[32]{0:T(128)} %constant.108) | copy-start | bytes 388
  294.9 10.4 %copy-start.2 = (f32[512]{0:T(512)S(1)}, f32[512]{0:T(512)}, u32[]{:S(2)}) copy-start(f32[512]{0:T(512)} %param.18) | copy-start | bytes 6148
  294.9 78.2 %copy-start.3 = (f32[2048]{0:T(1024)S(1)}, f32[2048]{0:T(1024)}, u32[]{:S(2)}) copy-start(f32[2048]{0:T(1024)} %param.17) | copy-start | bytes 24580
Sparse Core Ops, SparseCore 0:
  10.1 53.0 all-gather.8
  65.4 48.8 all-gather.6
  116.5 124.9 all-gather.10
  243.6 125.2 all-gather.12
